TPU v7x, 32 devices: a whole 2x2x4 slice. The times are simulated.
32 devices in a mesh: groups: 2 (over x), shard: 16 (over z, y, core).
Axes of the slice: x: 2, y: 2, z: 4, core: 2. Of those that a mesh axis runs over, the one named last changes fastest.
Arguments:
- features: bfloat16 [8192, 4096], P(('groups', 'shard')), parts along dimension 0, may hold values from -6 to 6
- cotangent: bfloat16 [8192, 4096], P(('groups', 'shard')), parts along dimension 0, may hold values from -0.029907227 to 0.029907227
- member_weight: bfloat16 [1024, 4096], P('shard'), may hold values from -0.1875 to 0.1875
- shared_weight: bfloat16 [256, 2048], P('shard'), may hold values from -0.375 to 0.375
- shared_coords: int32 [8, 2], replicated, may hold values from 0 to 15, as said below
Outputs:
- activated: bfloat16 [8192, 4096], P(('groups', 'shard')), parts along dimension 0
- member_grad: float32 [2048, 4096], P(('groups', 'shard')), parts along dimension 0
- shared_grad: float32 [512, 2048], P(('groups', 'shard')), parts along dimension 0
There are 2 independent parts, one for each index of `groups`. A program takes and returns all parts, laid end to end along the dimension named above; an argument that names none is the same for every part. Nothing has to cross between parts.
Inputs may be any that keep to these rules, and one draw needn't show every extreme that they name: `shared_coords`: the 8 pairs (row block, column block) are distinct, and none lies in a member's diagonal square: row block // 4 differs from column block // 4.
All inputs are finite; a program needn't handle non-finite values.
Results may differ from a plain program's by a relative error of at most 0.0029.
Values may be sent and summed in bfloat16 or wider, within the bound.
A program may use at most 128 MiB of HBM per device.

v0:
```python
import jax
import jax.numpy as jnp
from jax import lax
from jax.sharding import PartitionSpec as P

ROOT_HALF = 0.7071067811865476
INV_ROOT_TWO_PI = 0.3989422804014327


def gelu_slope(hidden):
    return 0.5 * (
        1.0 + jax.scipy.special.erf(hidden * ROOT_HALF)
    ) + hidden * INV_ROOT_TWO_PI * jnp.exp(-0.5 * hidden * hidden)


def member_product(inputs, weights):
    return lax.dot_general(
        inputs, weights, (((2,), (0,)), ((1,), (1,))), preferred_element_type=jnp.float32
    )


def per_device(features, cotangent, member_weight, shared_weight, shared_coords):
    shard_count = lax.axis_size("shard")
    token_rows = features.shape[0]
    width = features.shape[1]
    local_rows = member_weight.shape[0]
    member_width = local_rows * shard_count
    members = width // member_width
    block = shared_weight.shape[0] * shard_count
    shared_count = shared_coords.shape[0]
    grid = width // block
    row_blocks = shared_coords[:, 0]
    col_blocks = shared_coords[:, 1]
    col_onehot = (col_blocks[:, None] == jnp.arange(grid, dtype=jnp.int32)[None, :]).astype(
        jnp.float32
    )
    feat_members = features.reshape(token_rows, members, member_width)
    feat_blocks = jnp.take(features.reshape(token_rows, grid, block), row_blocks, axis=1)
    shared_full = lax.all_gather(shared_weight, "shard", axis=0, tiled=True)
    shared_blocks = shared_full.reshape(block, shared_count, block)
    member_full = lax.all_gather(member_weight, "shard", axis=0, tiled=True)
    member_out = member_product(
        feat_members, member_full.reshape(member_width, members, member_width)
    )
    shared_out = lax.dot_general(
        feat_blocks, shared_blocks, (((2,), (0,)), ((1,), (1,))), preferred_element_type=jnp.float32
    )
    placed = jnp.einsum("stj,sk->tkj", shared_out, col_onehot, precision=lax.Precision.HIGHEST)
    hidden = jnp.transpose(member_out, (1, 0, 2)).reshape(token_rows, width) + placed.reshape(
        token_rows, width
    )
    activated = jax.nn.gelu(hidden, approximate=False).astype(jnp.bfloat16)
    grad_hidden = (cotangent.astype(jnp.float32) * gelu_slope(hidden)).astype(jnp.bfloat16)
    grad_members = grad_hidden.reshape(token_rows, members, member_width)
    grad_blocks = jnp.take(grad_hidden.reshape(token_rows, grid, block), col_blocks, axis=1)
    shared_term = lax.dot_general(
        feat_blocks, grad_blocks, (((0,), (0,)), ((1,), (1,))), preferred_element_type=jnp.float32
    )
    shared_term = jnp.transpose(shared_term, (1, 0, 2)).reshape(block, shared_count * block)
    ratio = member_width // block
    folded = shared_term.reshape(member_width, shared_count * block // ratio)
    term = lax.dot_general(
        feat_members, grad_members, (((0,), (0,)), ((1,), (1,))), preferred_element_type=jnp.float32
    )
    joint = lax.psum_scatter(
        jnp.concatenate(
            [
                jnp.transpose(term, (1, 0, 2)).reshape(lax.axis_size("shard") * local_rows, width),
                folded,
            ],
            axis=1,
        ),
        "shard",
        scatter_dimension=0,
        tiled=True,
    )
    member_grad = joint[:, :width]
    shared_grad = joint[:, width:].reshape(local_rows // ratio, shared_count * block)
    return (activated, member_grad, shared_grad)


def solution(mesh):
    return jax.shard_map(
        per_device,
        mesh=mesh,
        in_specs=(
            P(("groups", "shard"), None),
            P(("groups", "shard"), None),
            P("shard", None),
            P("shard", None),
            P(),
        ),
        out_specs=(
            P(("groups", "shard"), None),
            P(("groups", "shard"), None),
            P(("groups", "shard"), None),
        ),
        check_vma=False,
    )
```

profile of v0, /device:TPU:0, one launch (start us, length us, event | category | flops | bytes accessed | tf_op | source)
XLA Modules:
  0.0 424.5 jit_solution(14927127992019022304)
XLA Ops:
  7.2 0.7 all-gather.5.cloned.1.call-update
  7.9 0.0 all-gather.3.cloned.1.call-start
  8.0 0.7 all-gather.3.cloned.1.call-update
  8.7 0.0 reduce-scatter.2.cloned.1.call-start
  8.7 4.1 copy.65
  12.8 2.5 copy.59
  15.3 3.9 copy.60
  19.2 2.2 gather_fusion
  21.5 29.3 %all-gather.5.cloned.1.call-done = bf16[256,2048]{1,0:T(8,128)(2,1)} async-done(((bf16[16,2048]{1,0:T(8,128)(2,1)}), bf16[256,2048]{1,0:T(8,128)(2,1)}) %all-gather.5.cloned.1.call-update) | async-done | bytes 1048592 | tf_op jit(solution)/shard_map/all_gather | solution.py:39
  50.8 2.3 copy.61
  53.1 1.7 fusion.23
  54.8 4.0 convolution_bitcast_fusion
  58.8 5.4 %copy.75 = f32[256,16,256]{0,2,1:T(8,128)} copy(f32[256,16,256]{2,1,0:T(8,128)} %convolution_bitcast_fusion) | data formatting | bytes 8388608 | tf_op jit(solution)/shard_map/reshape | solution.py:49
  64.2 62.6 %all-gather.3.cloned.1.call-done = bf16[1024,4096]{1,0:T(8,128)(2,1)} async-done(((bf16[64,4096]{1,0:T(8,128)(2,1)}), bf16[1024,4096]{1,0:T(8,128)(2,1)}) %all-gather.3.cloned.1.call-update) | async-done | bytes 8388624 | tf_op jit(solution)/shard_map/all_gather | solution.py:41
  126.9 11.9 %copy.55 = bf16[1024,4096]{0,1:T(8,128)(2,1)} copy(bf16[1024,4096]{1,0:T(8,128)(2,1)} %all-gather.3.cloned.1.call-done) | data formatting | bytes 16777216 | tf_op jit(solution)/shard_map/all_gather | solution.py:41
  138.8 7.7 %convolution_bitcast_fusion.1 = f32[256,4,1024]{2,0,1:T(8,128)} fusion(bf16[1024,4,1024]{0,2,1:T(8,128)(2,1)} %bitcast.55, bf16[32,4,8,1024]{3,2,1,0:T(8,128)(2,1)S(1)} %bitcast.56), kind=kOutput, calls=%fused_computation.30 | convolution fusion | flops 2147483648 | bytes 14680064 | tf_op jit(solution)/shard_map/dot_general | solution.py:17
  146.5 5.4 %copy.58 = f32[256,4,1024]{0,2,1:T(8,128)} copy(f32[256,4,1024]{2,0,1:T(8,128)} %convolution_bitcast_fusion.1) | data formatting | bytes 8388608 | tf_op jit(solution)/shard_map/transpose | solution.py:49
  151.9 13.5 %fusion.7 = (bf16[256,4096]{0,1:T(8,128)(2,1)}, bf16[256,4096]{0,1:T(8,128)(2,1)}) fusion(bf16[256,4096]{0,1:T(8,128)(2,1)} %copy.65, f32[256,16,256]{0,2,1:T(8,128)} %copy.75, f32[256,4,1024]{0,2,1:T(8,128)} %copy.58), kind=kLoop, calls=%fused_computation.12 | loop fusion | flops 80740352 | bytes 14680064 | tf_op jit(solution)/shard_map/convert_element_type | solution.py:53
  165.4 3.9 copy.67
  169.3 3.2 gather_fusion.1
  172.5 1.8 convolution_bitcast_fusion.2
  174.3 2.5 copy.69
  176.8 2.9 reshape_reshape.3
  179.7 9.7 %fusion.15 = f32[4,1024,1024]{2,1,0:T(8,128)} fusion(bf16[256,4,1024]{0,2,1:T(8,128)(2,1)} %bitcast.59, bf16[32,4,8,1024]{3,2,1,0:T(8,128)(2,1)S(1)} %bitcast.57), kind=kOutput, calls=%fused_computation.31 | convolution fusion | flops 2147483648 | bytes 20971520 | tf_op jit(solution)/shard_map/dot_general | solution.py:62
  189.4 17.6 %copy.70 = f32[1024,4096]{1,0:T(8,128)} copy(f32[1024,4096]{0,1:T(8,128)} %bitcast.54) | data formatting | bytes 33554432 | tf_op jit(solution)/shard_map/reshape | solution.py:68
  207.0 13.7 %pad_maximum_fusion = f32[1024,4608]{1,0:T(8,128)} fusion(f32[1024,512]{1,0:T(8,128)S(1)} %copy-done.2, f32[1024,4096]{1,0:T(8,128)} %copy.70), kind=kLoop, calls=%fused_computation.2 | loop fusion | flops 4718592 | bytes 37748736 | tf_op jit(solution)/shard_map/concatenate | solution.py:66
  220.8 1.6 copy-done.1
  222.3 2.8 copy.71
  225.2 188.9 %reduce-scatter.2.cloned.1.call-done = f32[64,4608]{1,0:T(8,128)} async-done(((f32[1024,4608]{1,0:T(8,128)}), f32[64,4608]{1,0:T(8,128)}) %reduce-scatter.2.cloned.1.call-update) | async-done | bytes 1179664 | tf_op jit(solution)/shard_map/reduce_scatter | solution.py:65
  414.1 0.9 slice.21
  415.0 0.7 reshape.50
  415.7 2.3 slice.20
  (13 shorter events, 0.1 us)
Async XLA Ops:
  7.2 5.6 %copy-start = (bf16[256,4096]{1,0:T(8,128)(2,1)S(1)}, bf16[256,4096]{1,0:T(8,128)(2,1)}, u32[]{:S(2)}) copy-start(bf16[256,4096]{1,0:T(8,128)(2,1)} %param.7) | copy-start | bytes 6291460
  7.2 43.7 %all-gather.5.cloned.1.call-start = ((), (), s32[]{:S(2)}) async-start(), calls=%async_computation.2 | async-start | bytes 1114112 | tf_op jit(solution)/shard_map/all_gather | solution.py:39
  7.9 118.9 %all-gather.3.cloned.1.call-start = ((), (), s32[]{:S(2)}) async-start(), calls=%async_computation.1 | async-start | bytes 8912896 | tf_op jit(solution)/shard_map/all_gather | solution.py:41
  8.7 405.5 %reduce-scatter.2.cloned.1.call-start = ((), (), s32[]{:S(2)}) async-start(), calls=%async_computation.3 | async-start | bytes 20054016 | tf_op jit(solution)/shard_map/reduce_scatter | solution.py:65
  12.8 6.4 %copy-start.3 = (s32[8,2]{0,1:T(2,128)S(1)}, s32[8,2]{0,1:T(2,128)}, u32[]{:S(2)}) copy-start(s32[8,2]{0,1:T(2,128)} %param.11) | copy-start | bytes 196
  189.4 17.6 %copy-start.2 = (f32[1024,512]{1,0:T(8,128)S(1)}, f32[1024,512]{1,0:T(8,128)}, u32[]{:S(2)}) copy-start(f32[1024,512]{1,0:T(8,128)} %reshape_reshape.3) | copy-start | bytes 6291460
  220.7 1.6 copy-start.1
Sparse Core Ops, SparseCore 0:
  10.2 40.6 all-gather.4
  53.0 73.8 all-gather.2
  220.9 193.1 reduce-scatter.1
where the time goes:
time: 426 us; the launch traced here: 425 us
  waiting for transfers between devices  282 us (66%)
  local copies, waits for them, and re-layouts  76.1 us (18%)
  other arithmetic  27.2 us (6%)
  matrix products  24.9 us (6%)
  between operations  13.8 us (3%)
    reduce_scatter x1, waiting for transfers between devices, per_device(): lax.psum_scatter(jnp.concatenate([jnp.transpose(term, (1, 0, 2)).reshape(...  189 us
    all_gather x1, waiting for transfers between devices, per_device(): member_full = lax.all_gather(member_weight, 'shard', axis=0, tiled=True)  62.6 us
    all_gather x1, waiting for transfers between devices, per_device(): shared_full = lax.all_gather(shared_weight, 'shard', axis=0, tiled=True)  29.3 us
    reshape x1, local copies, waits for them, and re-layouts, per_device(): jnp.transpose(term, (1, 0, 2))  17.6 us
    concatenate x1, other arithmetic, per_device(): jnp.concatenate([jnp.transpose(term, (1, 0, 2)).reshape(lax.axis_size('sh...  13.7 us
    convert_element_type x1, other arithmetic, per_device(): (cotangent.astype(jnp.float32) * gelu_slope(hidden)).astype(jnp.bfloat16)  13.5 us
    all_gather x1, local copies, waits for them, and re-layouts, per_device(): member_full = lax.all_gather(member_weight, 'shard', axis=0, tiled=True)  11.9 us
    unnamed x11, local copies, waits for them, and re-layouts  11 us
  transfers between devices with their start and end apart: 3, of which 3 were waited for; matrix products, arithmetic and copies ran while one was open for 7% of the time, Pallas kernels for 0%

commit v1 on v0

--- a/solution.py
+++ b/solution.py
@@ -5,6 +5,13 @@
 
 ROOT_HALF = 0.7071067811865476
 INV_ROOT_TWO_PI = 0.3989422804014327
+
+
+def solve_the_terms(x_in, along_dim):
+    x_in = jnp.moveaxis(x_in, 0, along_dim)
+    u1 = x_in.shape
+    new = x_in.reshape(*u1[:along_dim], u1[along_dim] * u1[along_dim + 1], *u1[along_dim + 2 :])
+    return new
 
 
 def gelu_slope(hidden):
@@ -36,7 +43,26 @@
     )
     feat_members = features.reshape(token_rows, members, member_width)
     feat_blocks = jnp.take(features.reshape(token_rows, grid, block), row_blocks, axis=1)
-    shared_full = lax.all_gather(shared_weight, "shard", axis=0, tiled=True)
+    n_lanes = lax.axis_size("shard")
+    all_rows = [(u, (u + 1) % n_lanes) for u in range(n_lanes)]
+    column = [(i0, to_i) for to_i, i0 in all_rows]
+    clean, answer = ([], [])
+    for at in range(n_lanes - 1):
+        if at % 2 == 0:
+            clean.append(
+                lax.ppermute(
+                    clean[-1] if clean else shared_weight, axis_name="shard", perm=all_rows
+                )
+            )
+        else:
+            newest = lax.ppermute(answer[-1] if answer else shared_weight, "shard", perm=column)
+            answer.append(newest)
+    inter = jnp.stack([*clean[::-1], shared_weight, *answer], axis=0)
+    current_block = len(clean)
+    long_array = lax.axis_index("shard")
+    s_next = long_array - current_block
+    inter = inter[(jnp.arange(n_lanes) - s_next) % n_lanes]
+    shared_full = solve_the_terms(inter, 0)
     shared_blocks = shared_full.reshape(block, shared_count, block)
     member_full = lax.all_gather(member_weight, "shard", axis=0, tiled=True)
     member_out = member_product(

time: 426 us -> 405 us (0.951)
  waiting for transfers between devices: 282 us -> 211 us
  starting transfers between devices: 0.11 us -> 32.4 us
  local copies, waits for them, and re-layouts: 76.1 us -> 93.8 us
    all_gather x1, waiting for transfers between devices: 62.6 us -> 0.01 us  [per_device(): member_full = lax.all_gather(member_weight, 'shard', axis=0, tiled=True)]
    ppermute x0 -> x15, starting transfers between devices: none -> 32.3 us  [the longest x7 31.8 us: per_device(): lax.ppermute(answer[-1] if answer else shared_weight, 'shard', perm=column)]
    all_gather x1 -> x0, waiting for transfers between devices: 29.3 us -> none  [per_device(): shared_full = lax.all_gather(shared_weight, 'shard', axis=0, tiled=True)]
    ppermute x0 -> x15, waiting for transfers between devices: none -> 21.9 us  [the longest x8 14.2 us: per_device(): lax.ppermute(clean[-1] if clean else shared_weight, axis_name='shard', pe...]
    unnamed x11 -> x31, local copies, waits for them, and re-layouts: 11 us -> 26.2 us
  transfers between devices with their start and end apart: 3 -> 17, of which waited for: 3 -> 11; matrix products, arithmetic and copies ran while one was open for 7% -> 12% of each run, Pallas kernels for 0% -> 0%
where the time goes in v1:
time: 405 us; the launch traced here: 403 us
  waiting for transfers between devices  211 us (52%)
  local copies, waits for them, and re-layouts  93.8 us (23%)
  starting transfers between devices  32.4 us (8%)
  other arithmetic  28 us (7%)
  matrix products  24 us (6%)
  between operations  14.1 us (3%)
    reduce_scatter x1, waiting for transfers between devices, per_device(): lax.psum_scatter(jnp.concatenate([jnp.transpose(term, (1, 0, 2)).reshape(...  188 us
    ppermute x7, starting transfers between devices, per_device(): lax.ppermute(answer[-1] if answer else shared_weight, 'shard', perm=column)  31.8 us
    unnamed x31, local copies, waits for them, and re-layouts  26.2 us
    reshape x1, local copies, waits for them, and re-layouts, per_device(): jnp.transpose(term, (1, 0, 2))  17.7 us
    ppermute x8, waiting for transfers between devices, per_device(): lax.ppermute(clean[-1] if clean else shared_weight, axis_name='shard', pe...  14.2 us
    concatenate x1, other arithmetic, per_device(): jnp.concatenate([jnp.transpose(term, (1, 0, 2)).reshape(lax.axis_size('sh...  13.7 us
    convert_element_type x1, other arithmetic, per_device(): (cotangent.astype(jnp.float32) * gelu_slope(hidden)).astype(jnp.bfloat16)  13.5 us
    all_gather x1, local copies, waits for them, and re-layouts, per_device(): member_full = lax.all_gather(member_weight, 'shard', axis=0, tiled=True)  11.7 us
  transfers between devices with their start and end apart: 17, of which 11 were waited for; matrix products, arithmetic and copies ran while one was open for 12% of the time, Pallas kernels for 0%

profile of v1, /device:TPU:0, one launch (start us, length us, event | category | flops | bytes accessed | tf_op | source)
XLA Modules:
  0.0 403.4 jit_solution(1280496311878032442)
XLA Ops:
  8.5 7.2 %collective-permute-done = bf16[16,2048]{1,0:T(8,128)(2,1)S(1)} collective-permute-done((bf16[16,2048]{1,0:T(8,128)(2,1)}, bf16[16,2048]{1,0:T(8,128)(2,1)S(1)}, u32[]{:S(2)}, u32[]{:S(2)}) %collective-permute-start) | collective-permute-done | bytes 65568 | tf_op jit(solution)/shard_map/ppermute | solution.py:53
  15.6 4.4 %collective-permute-start.8 = (bf16[16,2048]{1,0:T(8,128)(2,1)}, bf16[16,2048]{1,0:T(8,128)(2,1)S(1)}, u32[]{:S(2)}, u32[]{:S(2)}) collective-permute-start(bf16[16,2048]{1,0:T(8,128)(2,1)} %param.10), channel_id=1, source_target_pairs={{1,0},{2,1},{3,2},{4,3},{5,4},{6,5},{7,6},{8,7},{9,8},{10,9},{11,1... | collective-permute-start | bytes 196616 | tf_op jit(solution)/shard_map/ppermute | solution.py:58
  22.8 4.6 %collective-permute-start.9 = (bf16[16,2048]{1,0:T(8,128)(2,1)S(1)}, bf16[16,2048]{1,0:T(8,128)(2,1)S(1)}, u32[]{:S(2)}, u32[]{:S(2)}) collective-permute-start(bf16[16,2048]{1,0:T(8,128)(2,1)S(1)} %collective-permute-done.8), channel_id=1, source_target_pairs={{1,0},{2,1},{3,2},{4,3},{5,4},{6,5},{7,6},{8,7},{9,8},{10,9},{11,1... | collective-permute-start | bytes 196616 | tf_op jit(solution)/shard_map/ppermute | solution.py:58
  27.4 2.1 collective-permute-done.2
  30.5 4.6 %collective-permute-start.10 = (bf16[16,2048]{1,0:T(8,128)(2,1)S(1)}, bf16[16,2048]{1,0:T(8,128)(2,1)}, u32[]{:S(2)}, u32[]{:S(2)}) collective-permute-start(bf16[16,2048]{1,0:T(8,128)(2,1)S(1)} %collective-permute-done.9), channel_id=1, source_target_pairs={{1,0},{2,1},{3,2},{4,3},{5,4},{6,5},{7,6},{8,7},{9,8},{10,9},{11,1... | collective-permute-start | bytes 196616 | tf_op jit(solution)/shard_map/ppermute | solution.py:58
  35.2 2.1 collective-permute-done.3
  38.5 4.1 %copy.48 = bf16[256,4096]{0,1:T(8,128)(2,1)} copy(bf16[256,4096]{1,0:T(8,128)(2,1)} %param.8) | data formatting | bytes 4194304 | tf_op args[1]
  42.6 2.5 copy.43
  45.1 4.0 copy.44
  49.1 4.4 %collective-permute-start.11 = (bf16[16,2048]{1,0:T(8,128)(2,1)}, bf16[16,2048]{1,0:T(8,128)(2,1)}, u32[]{:S(2)}, u32[]{:S(2)}) collective-permute-start(bf16[16,2048]{1,0:T(8,128)(2,1)} %collective-permute-done.10), channel_id=1, source_target_pairs={{1,0},{2,1},{3,2},{4,3},{5,4},{6,5},{7,6},{8,7},{9,8},{10,9},{11,1... | collective-permute-start | bytes 196616 | tf_op jit(solution)/shard_map/ppermute | solution.py:58
  53.5 2.2 gather_fusion.1
  57.0 4.7 %collective-permute-start.12 = (bf16[16,2048]{1,0:T(8,128)(2,1)}, bf16[16,2048]{1,0:T(8,128)(2,1)S(1)}, u32[]{:S(2)}, u32[]{:S(2)}) collective-permute-start(bf16[16,2048]{1,0:T(8,128)(2,1)} %collective-permute-done.11), channel_id=1, source_target_pairs={{1,0},{2,1},{3,2},{4,3},{5,4},{6,5},{7,6},{8,7},{9,8},{10,9},{11,1... | collective-permute-start | bytes 196616 | tf_op jit(solution)/shard_map/ppermute | solution.py:58
  61.7 3.5 collective-permute-done.12
  65.1 4.5 %collective-permute-start.13 = (bf16[16,2048]{1,0:T(8,128)(2,1)S(1)}, bf16[16,2048]{1,0:T(8,128)(2,1)S(1)}, u32[]{:S(2)}, u32[]{:S(2)}) collective-permute-start(bf16[16,2048]{1,0:T(8,128)(2,1)S(1)} %collective-permute-done.12), channel_id=1, source_target_pairs={{1,0},{2,1},{3,2},{4,3},{5,4},{6,5},{7,6},{8,7},{9,8},{10,9},{11,1... | collective-permute-start | bytes 196616 | tf_op jit(solution)/shard_map/ppermute | solution.py:58
  71.5 4.6 %collective-permute-start.14 = (bf16[16,2048]{1,0:T(8,128)(2,1)S(1)}, bf16[16,2048]{1,0:T(8,128)(2,1)S(1)}, u32[]{:S(2)}, u32[]{:S(2)}) collective-permute-start(bf16[16,2048]{1,0:T(8,128)(2,1)S(1)} %collective-permute-done.13), channel_id=1, source_target_pairs={{1,0},{2,1},{3,2},{4,3},{5,4},{6,5},{7,6},{8,7},{9,8},{10,9},{11,1... | collective-permute-start | bytes 196616 | tf_op jit(solution)/shard_map/ppermute | solution.py:58
  91.4 3.0 gather_fusion
  96.4 4.2 %convolution_bitcast_fusion = f32[256,16,256]{2,1,0:T(8,128)} fusion(f32[8,256,256]{2,1,0:T(8,128)S(1)} %fusion.23, s32[8]{0:T(128)S(1)} %copy-done.5), kind=kOutput, calls=%fused_computation.30 | convolution fusion | flops 100663424 | bytes 6291488 | tf_op jit(solution)/shard_map/stj,sk->tkj/dot_general | solution.py:74
  100.6 5.2 %copy.57 = f32[256,16,256]{0,2,1:T(8,128)} copy(f32[256,16,256]{2,1,0:T(8,128)} %convolution_bitcast_fusion) | data formatting | bytes 8388608 | tf_op jit(solution)/shard_map/reshape | solution.py:75
  105.9 11.7 %copy.39 = bf16[1024,4096]{0,1:T(8,128)(2,1)} copy(bf16[1024,4096]{1,0:T(8,128)(2,1)} %all-gather.2.cloned.1.call-done) | data formatting | bytes 16777216 | tf_op jit(solution)/shard_map/all_gather | solution.py:67
  117.6 7.8 %convolution_bitcast_fusion.1 = f32[256,4,1024]{2,0,1:T(8,128)} fusion(bf16[1024,4,1024]{0,2,1:T(8,128)(2,1)} %bitcast.90, bf16[32,4,8,1024]{3,2,1,0:T(8,128)(2,1)S(1)} %bitcast.91), kind=kOutput, calls=%fused_computation.31 | convolution fusion | flops 2147483648 | bytes 14680064 | tf_op jit(solution)/shard_map/dot_general | solution.py:24
  125.4 5.4 %copy.42 = f32[256,4,1024]{0,2,1:T(8,128)} copy(f32[256,4,1024]{2,0,1:T(8,128)} %convolution_bitcast_fusion.1) | data formatting | bytes 8388608 | tf_op jit(solution)/shard_map/transpose | solution.py:75
  130.8 13.5 %fusion.7 = (bf16[256,4096]{0,1:T(8,128)(2,1)}, bf16[256,4096]{0,1:T(8,128)(2,1)}) fusion(bf16[256,4096]{0,1:T(8,128)(2,1)} %copy.48, f32[256,16,256]{0,2,1:T(8,128)} %copy.57, f32[256,4,1024]{0,2,1:T(8,128)} %copy.42), kind=kLoop, calls=%fused_computation.13 | loop fusion | flops 80740352 | bytes 14680064 | tf_op jit(solution)/shard_map/convert_element_type | solution.py:79
  144.3 3.9 copy.50
  148.2 3.2 gather_fusion.2
  153.2 2.5 copy.52
  155.7 2.9 reshape_reshape.7
  158.6 9.7 %fusion.15 = f32[4,1024,1024]{2,1,0:T(8,128)} fusion(bf16[256,4,1024]{0,2,1:T(8,128)(2,1)} %bitcast.94, bf16[32,4,8,1024]{3,2,1,0:T(8,128)(2,1)S(1)} %bitcast.92), kind=kOutput, calls=%fused_computation.32 | convolution fusion | flops 2147483648 | bytes 20971520 | tf_op jit(solution)/shard_map/dot_general | solution.py:88
  168.3 17.7 %copy.53 = f32[1024,4096]{1,0:T(8,128)} copy(f32[1024,4096]{0,1:T(8,128)} %bitcast.89) | data formatting | bytes 33554432 | tf_op jit(solution)/shard_map/reshape | solution.py:94
  186.0 13.7 %pad_maximum_fusion = f32[1024,4608]{1,0:T(8,128)} fusion(f32[1024,512]{1,0:T(8,128)S(1)} %copy-done.2, f32[1024,4096]{1,0:T(8,128)} %copy.53), kind=kLoop, calls=%fused_computation.3 | loop fusion | flops 4718592 | bytes 37748736 | tf_op jit(solution)/shard_map/concatenate | solution.py:92
  201.3 2.8 copy.54
  204.2 188.5 %reduce-scatter.2.cloned.1.call-done = f32[64,4608]{1,0:T(8,128)} async-done(((f32[1024,4608]{1,0:T(8,128)}), f32[64,4608]{1,0:T(8,128)}) %reduce-scatter.2.cloned.1.call-update) | async-done | bytes 1179664 | tf_op jit(solution)/shard_map/reduce_scatter | solution.py:91
  394.3 2.3 slice.22
  (62 shorter events, 31.9 us)
Async XLA Ops:
  7.2 35.4 %copy-start = (bf16[256,4096]{1,0:T(8,128)(2,1)S(1)}, bf16[256,4096]{1,0:T(8,128)(2,1)}, u32[]{:S(2)}) copy-start(bf16[256,4096]{1,0:T(8,128)(2,1)} %param.7) | copy-start | bytes 6291460
  7.2 98.7 %all-gather.2.cloned.1.call-start = ((), (), s32[]{:S(2)}) async-start(), calls=%async_computation.1 | async-start | bytes 8912896 | tf_op jit(solution)/shard_map/all_gather | solution.py:67
  7.9 384.7 %reduce-scatter.2.cloned.1.call-start = ((), (), s32[]{:S(2)}) async-start(), calls=%async_computation.2 | async-start | bytes 20054016 | tf_op jit(solution)/shard_map/reduce_scatter | solution.py:91
  8.0 7.7 %collective-permute-start = (bf16[16,2048]{1,0:T(8,128)(2,1)}, bf16[16,2048]{1,0:T(8,128)(2,1)S(1)}, u32[]{:S(2)}, u32[]{:S(2)}) collective-permute-start(bf16[16,2048]{1,0:T(8,128)(2,1)} %param.10), channel_id=1, source_target_pairs={{0,1},{1,2},{2,3},{3,4},{4,5},{5,6},{6,7},{7,8},{8,9},{9,10},{10,1... | collective-permute-start | bytes 196616 | tf_op jit(solution)/shard_map/ppermute | solution.py:53
  15.6 6.4 %collective-permute-start.1 = (bf16[16,2048]{1,0:T(8,128)(2,1)S(1)}, bf16[16,2048]{1,0:T(8,128)(2,1)S(1)}, u32[]{:S(2)}, u32[]{:S(2)}) collective-permute-start(bf16[16,2048]{1,0:T(8,128)(2,1)S(1)} %collective-permute-done), channel_id=1, source_target_pairs={{0,1},{1,2},{2,3},{3,4},{4,5},{5,6},{6,7},{7,8},{8,9},{9,10},{10,1... | collective-permute-start | bytes 196616 | tf_op jit(solution)/shard_map/ppermute | solution.py:53
  15.6 7.2 %collective-permute-start.8 = (bf16[16,2048]{1,0:T(8,128)(2,1)}, bf16[16,2048]{1,0:T(8,128)(2,1)S(1)}, u32[]{:S(2)}, u32[]{:S(2)}) collective-permute-start(bf16[16,2048]{1,0:T(8,128)(2,1)} %param.10), channel_id=1, source_target_pairs={{1,0},{2,1},{3,2},{4,3},{5,4},{6,5},{7,6},{8,7},{9,8},{10,9},{11,1... | collective-permute-start | bytes 196616 | tf_op jit(solution)/shard_map/ppermute | solution.py:58
  22.0 7.5 %collective-permute-start.2 = (bf16[16,2048]{1,0:T(8,128)(2,1)S(1)}, bf16[16,2048]{1,0:T(8,128)(2,1)S(1)}, u32[]{:S(2)}, u32[]{:S(2)}) collective-permute-start(bf16[16,2048]{1,0:T(8,128)(2,1)S(1)} %collective-permute-done.1), channel_id=1, source_target_pairs={{0,1},{1,2},{2,3},{3,4},{4,5},{5,6},{6,7},{7,8},{8,9},{9,10},{10,1... | collective-permute-start | bytes 196616 | tf_op jit(solution)/shard_map/ppermute | solution.py:53
  22.8 7.7 %collective-permute-start.9 = (bf16[16,2048]{1,0:T(8,128)(2,1)S(1)}, bf16[16,2048]{1,0:T(8,128)(2,1)S(1)}, u32[]{:S(2)}, u32[]{:S(2)}) collective-permute-start(bf16[16,2048]{1,0:T(8,128)(2,1)S(1)} %collective-permute-done.8), channel_id=1, source_target_pairs={{1,0},{2,1},{3,2},{4,3},{5,4},{6,5},{7,6},{8,7},{9,8},{10,9},{11,1... | collective-permute-start | bytes 196616 | tf_op jit(solution)/shard_map/ppermute | solution.py:58
  29.5 7.8 %collective-permute-start.3 = (bf16[16,2048]{1,0:T(8,128)(2,1)S(1)}, bf16[16,2048]{1,0:T(8,128)(2,1)S(1)}, u32[]{:S(2)}, u32[]{:S(2)}) collective-permute-start(bf16[16,2048]{1,0:T(8,128)(2,1)S(1)} %collective-permute-done.2), channel_id=1, source_target_pairs={{0,1},{1,2},{2,3},{3,4},{4,5},{5,6},{6,7},{7,8},{8,9},{9,10},{10,1... | collective-permute-start | bytes 196616 | tf_op jit(solution)/shard_map/ppermute | solution.py:53
  30.5 18.5 %collective-permute-start.10 = (bf16[16,2048]{1,0:T(8,128)(2,1)S(1)}, bf16[16,2048]{1,0:T(8,128)(2,1)}, u32[]{:S(2)}, u32[]{:S(2)}) collective-permute-start(bf16[16,2048]{1,0:T(8,128)(2,1)S(1)} %collective-permute-done.9), channel_id=1, source_target_pairs={{1,0},{2,1},{3,2},{4,3},{5,4},{6,5},{7,6},{8,7},{9,8},{10,9},{11,1... | collective-permute-start | bytes 196616 | tf_op jit(solution)/shard_map/ppermute | solution.py:58
  37.2 7.9 %copy-start.4 = (bf16[16,2048]{1,0:T(8,128)(2,1)}, bf16[16,2048]{1,0:T(8,128)(2,1)S(1)}, u32[]{:S(2)}) copy-start(bf16[16,2048]{1,0:T(8,128)(2,1)S(1)} %collective-permute-done.3) | copy-start | bytes 196612
  37.2 16.2 %collective-permute-start.4 = (bf16[16,2048]{1,0:T(8,128)(2,1)S(1)}, bf16[16,2048]{1,0:T(8,128)(2,1)}, u32[]{:S(2)}, u32[]{:S(2)}) collective-permute-start(bf16[16,2048]{1,0:T(8,128)(2,1)S(1)} %collective-permute-done.3), channel_id=1, source_target_pairs={{0,1},{1,2},{2,3},{3,4},{4,5},{5,6},{6,7},{7,8},{8,9},{9,10},{10,1... | collective-permute-start | bytes 196616 | tf_op jit(solution)/shard_map/ppermute | solution.py:53
  45.1 39.5 %copy-start.3 = (bf16[16,2048]{1,0:T(8,128)(2,1)S(1)}, bf16[16,2048]{1,0:T(8,128)(2,1)}, u32[]{:S(2)}) copy-start(bf16[16,2048]{1,0:T(8,128)(2,1)} %param.10) | copy-start | bytes 196612
  49.1 7.9 %collective-permute-start.11 = (bf16[16,2048]{1,0:T(8,128)(2,1)}, bf16[16,2048]{1,0:T(8,128)(2,1)}, u32[]{:S(2)}, u32[]{:S(2)}) collective-permute-start(bf16[16,2048]{1,0:T(8,128)(2,1)} %collective-permute-done.10), channel_id=1, source_target_pairs={{1,0},{2,1},{3,2},{4,3},{5,4},{6,5},{7,6},{8,7},{9,8},{10,9},{11,1... | collective-permute-start | bytes 196616 | tf_op jit(solution)/shard_map/ppermute | solution.py:58
  53.5 8.2 %collective-permute-start.5 = (bf16[16,2048]{1,0:T(8,128)(2,1)}, bf16[16,2048]{1,0:T(8,128)(2,1)}, u32[]{:S(2)}, u32[]{:S(2)}) collective-permute-start(bf16[16,2048]{1,0:T(8,128)(2,1)} %collective-permute-done.4), channel_id=1, source_target_pairs={{0,1},{1,2},{2,3},{3,4},{4,5},{5,6},{6,7},{7,8},{8,9},{9,10},{10,1... | collective-permute-start | bytes 196616 | tf_op jit(solution)/shard_map/ppermute | solution.py:53
  57.0 8.1 %collective-permute-start.12 = (bf16[16,2048]{1,0:T(8,128)(2,1)}, bf16[16,2048]{1,0:T(8,128)(2,1)S(1)}, u32[]{:S(2)}, u32[]{:S(2)}) collective-permute-start(bf16[16,2048]{1,0:T(8,128)(2,1)} %collective-permute-done.11), channel_id=1, source_target_pairs={{1,0},{2,1},{3,2},{4,3},{5,4},{6,5},{7,6},{8,7},{9,8},{10,9},{11,1... | collective-permute-start | bytes 196616 | tf_op jit(solution)/shard_map/ppermute | solution.py:58
  61.7 8.0 %collective-permute-start.6 = (bf16[16,2048]{1,0:T(8,128)(2,1)}, bf16[16,2048]{1,0:T(8,128)(2,1)S(1)}, u32[]{:S(2)}, u32[]{:S(2)}) collective-permute-start(bf16[16,2048]{1,0:T(8,128)(2,1)} %collective-permute-done.5), channel_id=1, source_target_pairs={{0,1},{1,2},{2,3},{3,4},{4,5},{5,6},{6,7},{7,8},{8,9},{9,10},{10,1... | collective-permute-start | bytes 196616 | tf_op jit(solution)/shard_map/ppermute | solution.py:53
  65.1 6.4 %collective-permute-start.13 = (bf16[16,2048]{1,0:T(8,128)(2,1)S(1)}, bf16[16,2048]{1,0:T(8,128)(2,1)S(1)}, u32[]{:S(2)}, u32[]{:S(2)}) collective-permute-start(bf16[16,2048]{1,0:T(8,128)(2,1)S(1)} %collective-permute-done.12), channel_id=1, source_target_pairs={{1,0},{2,1},{3,2},{4,3},{5,4},{6,5},{7,6},{8,7},{9,8},{10,9},{11,1... | collective-permute-start | bytes 196616 | tf_op jit(solution)/shard_map/ppermute | solution.py:58
  69.6 7.4 %collective-permute-start.7 = (bf16[16,2048]{1,0:T(8,128)(2,1)S(1)}, bf16[16,2048]{1,0:T(8,128)(2,1)S(1)}, u32[]{:S(2)}, u32[]{:S(2)}) collective-permute-start(bf16[16,2048]{1,0:T(8,128)(2,1)S(1)} %collective-permute-done.6), channel_id=1, source_target_pairs={{0,1},{1,2},{2,3},{3,4},{4,5},{5,6},{6,7},{7,8},{8,9},{9,10},{10,1... | collective-permute-start | bytes 196616 | tf_op jit(solution)/shard_map/ppermute | solution.py:53
  71.5 19.2 %collective-permute-start.14 = (bf16[16,2048]{1,0:T(8,128)(2,1)S(1)}, bf16[16,2048]{1,0:T(8,128)(2,1)S(1)}, u32[]{:S(2)}, u32[]{:S(2)}) collective-permute-start(bf16[16,2048]{1,0:T(8,128)(2,1)S(1)} %collective-permute-done.13), channel_id=1, source_target_pairs={{1,0},{2,1},{3,2},{4,3},{5,4},{6,5},{7,6},{8,7},{9,8},{10,9},{11,1... | collective-permute-start | bytes 196616 | tf_op jit(solution)/shard_map/ppermute | solution.py:58
  91.4 5.0 %copy-start.5 = (s32[8]{0:T(128)S(1)}, s32[8]{0:T(128)}, u32[]{:S(2)}) copy-start(s32[8]{0:T(128)} %slice_bitcast_fusion) | copy-start | bytes 100
  168.3 17.7 %copy-start.2 = (f32[1024,512]{1,0:T(8,128)S(1)}, f32[1024,512]{1,0:T(8,128)}, u32[]{:S(2)}) copy-start(f32[1024,512]{1,0:T(8,128)} %reshape_reshape.7) | copy-start | bytes 6291460
  199.7 1.6 copy-start.1
Sparse Core Ops, SparseCore 0:
  10.2 82.8 all-gather.1
  199.9 192.7 reduce-scatter.1
